TPU v7x, 32 devices: a whole 2x2x4 slice. The times are simulated.
32 devices in a mesh: batch: 2 (over y), res: 16 (over z, x, core), head: 1.
Axes of the slice: x: 2, y: 2, z: 4, core: 2. Of those that a mesh axis runs over, the one named last changes fastest.
Arguments:
- single: bfloat16 [768, 384], P(('batch', 'res')), parts along dimension 0, may hold values from -50 to 50
- pair: bfloat16 [768, 384, 128], P(('batch', 'res'), 'head'), parts along dimension 0, may hold values from -6 to 6
- rotations: float32 [3, 3, 768], P(None, None, 'batch'), parts along dimension 2, may hold values from -1 to 1, as said below
- translations: float32 [3, 768], P(None, 'batch'), parts along dimension 1, may hold values from -4 to 4
- residue_chain_index: int32 [384], replicated, may hold values from 0 to 3, never falling along the last dimension, each value on 1 to 192 neighbouring positions
- residue_move_mask: int32 [768], P('batch'), parts along dimension 0, may hold values 0 or 1
- timestep: int32 [1], replicated, may hold values from 0 to 6
- single_projection_weight: bfloat16 [384, 16, 132], P(None, 'head'), may hold values from -1 to 1, as said below
- head_bias_weight: bfloat16 [128, 16], replicated, may hold values from -0.5 to 0.5
- head_distance_weight: float32 [16], P('head'), may hold values from 0.1 to 1
- chain_logit_offset: float32 [16], P('head'), may hold values from -2 to 2
- local_output_weight: bfloat16 [16, 64, 384], P('head'), may hold values from -0.109375 to 0.109375
- pair_output_weight: bfloat16 [16, 128, 384], replicated, may hold values from -0.109375 to 0.109375
- single_norm_gain: float32 [384], replicated, may hold values from 0.5 to 1.5
- frame_velocity_weight: bfloat16 [384, 6], replicated, may hold values from -0.3125 to 0.3125
- left_pair_weight: bfloat16 [384, 128], replicated, may hold values from -0.3125 to 0.3125
- right_pair_weight: bfloat16 [384, 128], replicated, may hold values from -0.3125 to 0.3125
- pair_norm_gain: float32 [128], replicated, may hold values from 0.5 to 1.5
- transition_hidden_weight: bfloat16 [128, 256], replicated, may hold values from -0.5 to 0.5
- transition_middle_weight: bfloat16 [256, 256], replicated, may hold values from -0.375 to 0.375
- transition_back_weight: bfloat16 [256, 128], replicated, may hold values from -0.375 to 0.375
Outputs:
- single_out: bfloat16 [768, 384], P(('batch', 'res')), parts along dimension 0
- rot_out: float32 [3, 3, 768], P(None, None, ('batch', 'res')), parts along dimension 2
- trans_out: float32 [3, 768], P(None, ('batch', 'res')), parts along dimension 1
- pair_out: bfloat16 [768, 384, 128], P(('batch', 'res'), 'head'), parts along dimension 0
There are 2 independent parts, one for each index of `batch`. A program takes and returns all parts, laid end to end along the dimension named above; an argument that names none is the same for every part. Nothing has to cross between parts.
Inputs may be any that keep to these rules, and one draw needn't show every extreme that they name: Each residue's 3 x 3 block rotations[:, :, i] is a rotation matrix. `single_projection_weight`: mean zero entries of deviation about 1 / sqrt(384).
All inputs are finite; a program needn't handle non-finite values.
Results may differ from a plain program's by a relative error of at most 0.0044.
The roundings to bfloat16 on the way count: a program that leaves them out, or rounds other values in their place, can miss the bound.
Values may be sent and summed in bfloat16 or wider, within the bound.
A program may use at most 64 MiB of HBM per device.

v0:
```python
import math

import jax
import jax.numpy as jnp
from jax import lax
from jax.experimental import pallas as pl
from jax.experimental.pallas import tpu as pltpu
from jax.sharding import PartitionSpec as P

HEAD_FEATURES = 16
PQ = 8
PV = 12
STEPS = 8


LOGIT_FACTOR = math.sqrt(1.0 / 3.0)
HIGHEST = lax.Precision.HIGHEST


def rounded(values):
    return lax.optimization_barrier(values.astype(jnp.bfloat16))


def layer_norm(values, gain):
    centre = jnp.mean(values, axis=-1, keepdims=True)
    variance = jnp.mean(jnp.square(values - centre), axis=-1, keepdims=True)
    return (values - centre) * lax.rsqrt(variance + 1e-05) * gain


def to_global(local, rot_cols, trans_cols, npoints):
    rows_here = local.shape[0]
    heads_here = local.shape[1]
    points = local.reshape(rows_here, heads_here, npoints, 3)
    turned = jnp.sum(rot_cols[:, None, None, :, :] * points[:, :, :, None, :], axis=-1)
    return turned + trans_cols[:, None, None, :]


def key_features(projected, rot_cols, trans_cols):
    rows_here = projected.shape[0]
    heads_here = projected.shape[1]
    offset = 3 * HEAD_FEATURES
    key_points = to_global(
        projected[:, :, offset + 3 * PQ : offset + 6 * PQ], rot_cols, trans_cols, PQ
    )
    value_points = to_global(projected[:, :, offset + 6 * PQ :], rot_cols, trans_cols, PV)
    packed_projection = jnp.concatenate(
        [
            projected[:, :, HEAD_FEATURES : 3 * HEAD_FEATURES],
            key_points.reshape(rows_here, heads_here, 3 * PQ),
            value_points.reshape(rows_here, heads_here, 3 * PV),
        ],
        axis=-1,
    )
    return rounded(
        packed_projection.reshape(rows_here, heads_here * (2 * HEAD_FEATURES + 3 * PQ + 3 * PV))
    )


def hat_matrix(vectors):
    comp_x = vectors[:, 0]
    comp_y = vectors[:, 1]
    comp_z = vectors[:, 2]
    zeros_col = jnp.zeros_like(comp_x)
    first_row = jnp.stack([zeros_col, -comp_z, comp_y], -1)
    second_row = jnp.stack([comp_z, zeros_col, -comp_x], -1)
    third_row = jnp.stack([-comp_y, comp_x, zeros_col], -1)
    return jnp.stack([first_row, second_row, third_row], 1)


def frame_step(single_out, frame_velocity_weight, rot_cols, trans_cols, live_rows, step_ratio):
    motion = jnp.dot(single_out, frame_velocity_weight, preferred_element_type=jnp.float32)
    rotvec = step_ratio * jnp.tanh(motion[:, 0:3]) * live_rows[:, None]
    velocity = step_ratio * motion[:, 3:6] * live_rows[:, None]
    angle_sq = jnp.sum(jnp.square(rotvec), -1)
    coef_a = jnp.zeros_like(angle_sq)
    coef_b = jnp.zeros_like(angle_sq)
    coef_c = jnp.zeros_like(angle_sq)
    powers = jnp.ones_like(angle_sq)
    for order in range(8):
        parity = (-1.0) ** order
        coef_a = coef_a + powers * (parity / float(math.factorial(2 * order + 1)))
        coef_b = coef_b + powers * (parity / float(math.factorial(2 * order + 2)))
        coef_c = coef_c + powers * (parity / float(math.factorial(2 * order + 3)))
        powers = powers * angle_sq
    cross_mat = hat_matrix(rotvec)
    cross_sq = jnp.einsum("nab,nbc->nac", cross_mat, cross_mat, precision=HIGHEST)
    identity = jnp.eye(3, dtype=jnp.float32)[None]
    turn = identity + coef_a[:, None, None] * cross_mat + coef_b[:, None, None] * cross_sq
    jacobian = identity + coef_b[:, None, None] * cross_mat + coef_c[:, None, None] * cross_sq
    new_rot = jnp.einsum("nab,nbc->nac", rot_cols, turn, precision=HIGHEST)
    moved = jnp.einsum("nab,nb->na", jacobian, velocity, precision=HIGHEST)
    new_trans = trans_cols + jnp.einsum("nab,nb->na", rot_cols, moved, precision=HIGHEST)
    return (jnp.transpose(new_rot, (1, 2, 0)), jnp.transpose(new_trans))


def local_logit_rows(
    query_values,
    query_flattened,
    packed_projection,
    pair_head_bias,
    within_chain,
    distance_weight,
    chain_offset,
    key_present,
):
    key_scalar = packed_projection[:, :, 0:HEAD_FEATURES]
    key_flat = packed_projection[:, :, 2 * HEAD_FEATURES : 2 * HEAD_FEATURES + 3 * PQ].astype(
        jnp.float32
    )
    scalar_logit_term = jnp.einsum(
        "rhc,nhc->rhn", query_values, key_scalar, preferred_element_type=jnp.float32
    )
    cross_term = jnp.einsum("rhp,nhp->rhn", query_flattened, key_flat, precision=HIGHEST)
    key_square = jnp.transpose(jnp.sum(jnp.square(key_flat), -1))
    point_distance = (
        jnp.sum(jnp.square(query_flattened), -1)[:, :, None] + key_square[None] - 2.0 * cross_term
    )
    point_term_weight = math.sqrt(2.0 / (9.0 * PQ))
    logit_matrix = LOGIT_FACTOR * (
        scalar_logit_term / math.sqrt(HEAD_FEATURES)
        + pair_head_bias
        + chain_offset[None, :, None] * within_chain[:, None, :]
        - (0.5 * point_term_weight * distance_weight)[None, :, None] * point_distance
    )
    return jnp.where(key_present[None, None, :], logit_matrix, -1000000000.0)


def local_points(scalar_out, point_global, rot_own, trans_own, local_output_weight):
    rows_dev = scalar_out.shape[0]
    heads_here = scalar_out.shape[1]
    point_global = point_global.reshape(rows_dev, heads_here, PV, 3)
    centred = point_global - trans_own[:, None, None, :]
    point_local = jnp.sum(rot_own[:, None, None, :, :] * centred[:, :, :, :, None], axis=-2)
    point_norm = jnp.sqrt(jnp.sum(jnp.square(point_local), -1) + 1.0)
    features = jnp.concatenate(
        [scalar_out, point_local.reshape(rows_dev, heads_here, 3 * PV), point_norm], -1
    )
    return jnp.einsum(
        "rhf,hfd->rd", features, local_output_weight.astype(jnp.float32), precision=HIGHEST
    )


def push_blocks(src, buf, send_a, recv_a, send_b, recv_b):
    count = buf.shape[0]
    pairs = count // 2
    me = lax.axis_index("res")
    side = lax.rem(me, 2)
    chip = me // 2
    partner = chip * 2 + 1 - side

    def outgoing(step):
        target = partner if step == 0 else lax.rem(chip + step, pairs) * 2 + side
        return pltpu.make_async_remote_copy(
            src_ref=src,
            dst_ref=buf.at[me],
            send_sem=send_a.at[step],
            recv_sem=recv_a.at[step],
            device_id={"res": target},
            device_id_type=pl.DeviceIdType.MESH,
        )

    def passed_on(step):
        origin = lax.rem(chip + pairs - step, pairs) * 2 + side
        return pltpu.make_async_remote_copy(
            src_ref=buf.at[origin],
            dst_ref=buf.at[origin],
            send_sem=send_b.at[step],
            recv_sem=recv_b.at[step],
            device_id={"res": partner},
            device_id_type=pl.DeviceIdType.MESH,
        )

    def start():
        for step in range(1, pairs):
            outgoing(step).start()
        outgoing(0).start()
        buf[me] = src[...]

    def finish():
        for step in range(1, pairs):
            outgoing(step).wait_recv()
            passed_on(step).start()
        outgoing(0).wait_recv()
        for step in range(1, pairs):
            passed_on(step).wait_recv()
        for step in range(pairs):
            outgoing(step).wait_send()
        for step in range(1, pairs):
            passed_on(step).wait_send()

    return start, finish


def greet(count):
    pairs = count // 2
    me = lax.axis_index("res")
    side = lax.rem(me, 2)
    chip = me // 2
    barrier = pltpu.get_barrier_semaphore()
    for step in range(pairs):
        target = chip * 2 + 1 - side if step == 0 else lax.rem(chip + step, pairs) * 2 + side
        pl.semaphore_signal(
            barrier, inc=1, device_id={"res": target}, device_id_type=pl.DeviceIdType.MESH
        )
    pl.semaphore_wait(barrier, pairs)


def gather_kernel(src, out, buf, send_a, recv_a, send_b, recv_b):
    greet(buf.shape[0])
    start, finish = push_blocks(src, buf, send_a, recv_a, send_b, recv_b)
    start()
    finish()
    out[...] = buf[...]


def gather_blocks(block, count, collective_id):
    pairs = count // 2
    return pl.pallas_call(
        gather_kernel,
        out_shape=jax.ShapeDtypeStruct((count,) + block.shape, block.dtype),
        in_specs=[pl.BlockSpec(memory_space=pltpu.VMEM)],
        out_specs=pl.BlockSpec(memory_space=pltpu.VMEM),
        scratch_shapes=[pltpu.VMEM((count,) + block.shape, block.dtype)]
        + [pltpu.SemaphoreType.DMA((pairs,))] * 4,
        compiler_params=pltpu.CompilerParams(collective_id=collective_id, has_side_effects=True),
        name="gather_blocks",
    )(block)


def transition_kernel(
    live_rows, pair, left, right, live_cols, gain, first, middle, back, *rest
):
    *rest, wide = rest
    out = rest[len(rest) // 2]
    block = pair.shape[0]
    step = pl.program_id(0)
    own_start = lax.axis_index("res") * left.shape[0]

    @pl.when(step == 0)
    def _():
        live = jnp.where(live_cols[...] > 0, 1.0, 0.0)[None]
        wide[...] = jnp.transpose(jnp.broadcast_to(live, (wide.shape[1], wide.shape[0])))
        for src, dst in zip(rest[: len(rest) // 2], rest[len(rest) // 2 + 1 :]):
            dst[...] = src[...]

    cols, channels = pair.shape[1:]
    group = math.gcd(block, STACK)
    for row in range(0, block, group):
        stack = []
        for i in range(row, row + group):
            own = pair[i].astype(jnp.float32)
            summed = own + left[pl.ds(step * block + i, 1), :] + right[...]
            stack.append(layer_norm(summed, gain[...][None]).astype(jnp.bfloat16))
        normed = jnp.concatenate(stack, axis=0)
        hidden = jnp.dot(normed, first[...], preferred_element_type=jnp.float32)
        hidden = jnp.maximum(hidden.astype(jnp.bfloat16), 0)
        hidden = jnp.dot(hidden, middle[...], preferred_element_type=jnp.float32)
        hidden = jnp.maximum(hidden.astype(jnp.bfloat16), 0)
        branch = jnp.dot(hidden, back[...], preferred_element_type=jnp.float32)
        for i in range(row, row + group):
            live = jnp.where(live_rows[own_start + step * block + i] > 0, 1.0, 0.0)
            part = branch[(i - row) * cols : (i - row + 1) * cols]
            out[i] = (pair[i].astype(jnp.float32) + (live * wide[...]) * part).astype(jnp.bfloat16)


def run_transition(live_rows, pair, left, right, live_cols, gain, first, middle, back, *passed):
    rows, cols, channels = pair.shape
    block = math.gcd(rows, 12)
    whole = lambda a: pl.BlockSpec(a.shape, lambda i: (0,) * a.ndim)
    blocked = pl.BlockSpec((block, cols, channels), lambda i: (i, 0, 0))
    result = pl.pallas_call(
        transition_kernel,
        grid=(rows // block,),
        out_shape=[jax.ShapeDtypeStruct(a.shape, a.dtype) for a in (pair,) + passed],
        in_specs=[pl.BlockSpec(memory_space=pltpu.SMEM), blocked]
        + [whole(a) for a in (left, right, live_cols, gain, first, middle, back) + passed],
        out_specs=[blocked] + [whole(a) for a in passed],
        scratch_shapes=[pltpu.VMEM((cols, channels), jnp.float32)],
        name="transition",
    )(live_rows, pair, left, right, live_cols, gain, first, middle, back, *passed)
    return tuple(result[1:]) + (result[0],)


ROWS = 88
STACK = 4
GROUP = 4
FEAT = 80
NT = (((1,), (1,)), ((), ()))


def dot_nt(a, b):
    return lax.dot_general(a, b, NT, preferred_element_type=jnp.float32)


def lanes(ref, start, size, stride=1):
    at = pl.ds(start, size) if stride == 1 else pl.ds(start, size, stride)
    return jnp.concatenate([ref[c, at, :] for c in range(ref.shape[0])], axis=1)


def in_three(values):
    first = values.astype(jnp.bfloat16)
    rest = values - first.astype(jnp.float32)
    second = rest.astype(jnp.bfloat16)
    third = (rest - second.astype(jnp.float32)).astype(jnp.bfloat16)
    return first, second, third


def exact_dot(values, weight):
    return sum(
        jnp.dot(part, weight, preferred_element_type=jnp.float32)
        for part in reversed(in_three(values))
    )


def turned_planes(planes, frame, transpose=False):
    out = []
    for a in range(3):
        rows = [3 * b + a if transpose else 3 * a + b for b in range(3)]
        out.append(
            frame[rows[0] : rows[0] + 1] * planes[0]
            + frame[rows[1] : rows[1] + 1] * planes[1]
            + frame[rows[2] : rows[2] + 1] * planes[2]
        )
    return out


def attention_kernel(
    timestep,
    distance_weight,
    chain_offset,
    single,
    rotations,
    translations,
    chain,
    mask,
    bias_weight,
    norm_gain,
    velocity_weight,
    left_weight,
    right_weight,
    pair_hbm,
    proj_hbm,
    local_hbm,
    attended_hbm,
    single_out,
    rot_out,
    trans_out,
    left_out,
    right_out,
    buf,
    right_buf,
    right_own,
    pair,
    proj,
    local,
    attended,
    frames,
    proj_all,
    proj_own,
    query_t,
    point_t,
    placed_t,
    squares,
    bias,
    attn,
    local_wide,
    local_planes,
    features,
    pair_rows,
    sems,
    send_a,
    recv_a,
    send_b,
    recv_b,
    send_c,
    recv_c,
    send_d,
    recv_d,
):
    rows = single.shape[0]
    members = buf.shape[0]
    total = members * rows
    heads = bias_weight.shape[0]
    chunks = total // 128
    width = single.shape[1]
    shift = lax.rem(total - lax.axis_index("res") * rows, total)

    loads = [
        pltpu.make_async_copy(src, dst, sems.at[i])
        for i, (src, dst) in enumerate(
            [(proj_hbm, proj), (pair_hbm, pair), (local_hbm, local), (attended_hbm, attended)]
        )
    ]
    for load in loads:
        load.start()
    greet(members)
    start, finish = push_blocks(single, buf, send_a, recv_a, send_b, recv_b)
    start()

    for a in range(3):
        frames[3 * a : 3 * a + 3, :] = rotations[a]
    frames[9:12, :] = translations[...]
    frames[12:13, :] = chain[...].astype(jnp.float32)[None]
    frames[13:14, :] = jnp.where(mask[...] > 0, 1.0, 0.0)[None]
    frames[14:16, :] = jnp.zeros((2, total), jnp.float32)
    own_wide = pltpu.roll(frames[...], shift, 1)[:, 0:128]
    own = own_wide[:, 0:rows]
    own_cols = jnp.transpose(own_wide)[0:rows]
    within = jnp.where(own_cols[:, 12:13] == frames[12:13, :], 1.0, 0.0)
    present = jnp.broadcast_to(frames[13:14, :], (rows, total)) > 0

    loads[0].wait()
    proj_own[:, 0:rows] = dot_nt(proj[...], single[...])
    for h in range(heads):
        query_t[h * 16 : h * 16 + 16, :] = proj_own[pl.ds(h, 16, heads), :]
    for p in range(PQ):
        planes = [
            proj_own[(48 + 3 * p + c) * heads : (49 + 3 * p + c) * heads, :] for c in range(3)
        ]
        for c, plane in enumerate(turned_planes(planes, own_wide)):
            point_t[pl.ds(3 * p + c, heads, 3 * PQ), :] = plane + own_wide[9 + c : 10 + c]
    queries = jnp.transpose(query_t[...])[0:rows].astype(jnp.bfloat16)
    points = jnp.transpose(point_t[...])[0:rows]
    point_parts = in_three(points)
    for c in range(chunks):
        for at in (36, 52, 68):
            for i in range(4):
                placed_t[c, pl.ds(at + i, heads, ROWS), :] = jnp.zeros((heads, 128), jnp.float32)

    loads[1].wait()
    bias_t = bias_weight[...]
    for r in range(rows):
        row = dot_nt(bias_t, pair[r]).astype(jnp.bfloat16).astype(jnp.float32)
        for c in range(chunks):
            bias[c, r * heads : (r + 1) * heads, :] = row[:, c * 128 : (c + 1) * 128]

    loads[2].wait()
    for c in range(width // 128):
        local_wide[c, 0 : heads * 64, :] = local[:, c * 128 : (c + 1) * 128].astype(jnp.float32)
        local_wide[c, heads * 64 : heads * 64 + 8, :] = jnp.zeros((8, 128), jnp.float32)
    keep = lax.broadcasted_iota(jnp.int32, (16, width), 0) < PV
    for h in range(heads):
        base, at = h * 64, h * FEAT
        local_planes[at : at + 16, :] = local[base : base + 16, :]
        for c in range(3):
            plane = lanes(local_wide, base + 16 + c, 16, 3)
            local_planes[at + 16 * (c + 1) : at + 16 * (c + 2), :] = jnp.where(
                keep, plane, 0.0
            ).astype(jnp.bfloat16)
        plane = lanes(local_wide, base + 52, 16)
        local_planes[at + 64 : at + 80, :] = jnp.where(keep, plane, 0.0).astype(jnp.bfloat16)
    loads[3].wait()

    finish()
    every = buf[...].astype(jnp.float32).reshape(total, width).astype(jnp.bfloat16)
    for c in range(chunks):
        proj_all[c] = dot_nt(proj[...], every[c * 128 : (c + 1) * 128])

    frame = frames[...]
    key_square = jnp.zeros((heads, total), jnp.float32)
    for p in range(PQ + PV):
        at = 72 + 3 * p
        planes = [lanes(proj_all, (at + c) * heads, heads) for c in range(3)]
        for c, plane in enumerate(turned_planes(planes, frame)):
            plane = (plane + frame[9 + c : 10 + c]).astype(jnp.bfloat16).astype(jnp.float32)
            if p < PQ:
                key_square = key_square + plane * plane
                slot = 3 * p + c
            else:
                slot = 24 + 16 * c + p - PQ
            for k in range(chunks):
                placed_t[k, pl.ds(slot, heads, ROWS), :] = plane[:, k * 128 : (k + 1) * 128]
    squares[...] = key_square

    for group in range(0, heads, GROUP):
        members_here = range(group, group + GROUP)
        logits = []
        for h in members_here:
            base = h * ROWS
            keys = lanes(proj_all, 16 * heads + h, 16, heads).astype(jnp.bfloat16)
            key_points = lanes(placed_t, base, 24).astype(jnp.bfloat16)
            query_points = points[:, h * 24 : h * 24 + 24]
            query_square = jnp.sum(query_points * query_points, axis=1, keepdims=True)
            stacked = jnp.concatenate(
                [part[:, h * 24 : h * 24 + 24] for part in point_parts], axis=0
            )
            cross = jnp.dot(stacked, key_points, preferred_element_type=jnp.float32)
            cross = cross[2 * rows : 3 * rows] + cross[rows : 2 * rows] + cross[0:rows]
            distance = query_square + squares[h : h + 1, :] - 2.0 * cross
            scalar = jnp.dot(
                queries[:, h * 16 : h * 16 + 16], keys, preferred_element_type=jnp.float32
            )
            logit = LOGIT_FACTOR * (
                scalar * (1.0 / math.sqrt(HEAD_FEATURES))
                + lanes(bias, h, rows, heads)
                + chain_offset[h] * within
                - (0.5 * math.sqrt(2.0 / (9.0 * PQ)) * distance_weight[h]) * distance
            )
            logits.append(jnp.where(present, logit, -1000000000.0))
        peaks = [jnp.max(logit, axis=1, keepdims=True) for logit in logits]
        exponents = [jnp.exp(logit - peak) for logit, peak in zip(logits, peaks)]
        sums = [jnp.sum(exponent, axis=1, keepdims=True) for exponent in exponents]
        attended_by = [
            (exponent / amount).astype(jnp.bfloat16) for exponent, amount in zip(exponents, sums)
        ]
        for h, weights in zip(members_here, attended_by):
            wide = weights.astype(jnp.float32)
            for c in range(chunks):
                attn[c, pl.ds(h, rows, heads), :] = wide[:, c * 128 : (c + 1) * 128]
        results = []
        for h, weights in zip(members_here, attended_by):
            values = lanes(proj_all, 32 * heads + h, 16, heads)
            stack = jnp.concatenate([values, lanes(placed_t, h * ROWS + 24, 48)], axis=0)
            results.append(dot_nt(stack.astype(jnp.bfloat16), weights))
        for h, result in zip(members_here, results):
            at = h * FEAT
            features[at : at + 16, 0:rows] = result[0:16]
            centred = [
                result[16 * (c + 1) : 16 * (c + 2)] - own[9 + c : 10 + c] for c in range(3)
            ]
            placed = turned_planes(centred, own, transpose=True)
            square = placed[0] * placed[0] + placed[1] * placed[1] + placed[2] * placed[2]
            for c in range(3):
                features[at + 16 * (c + 1) : at + 16 * (c + 2), 0:rows] = placed[c]
            features[at + 64 : at + 80, 0:rows] = jnp.sqrt(square + 1.0)

    for r in range(rows):
        weights = lanes(attn, r * heads, heads).astype(jnp.bfloat16)
        pair_rows[r * heads : (r + 1) * heads, :] = jnp.dot(
            weights, pair[r], preferred_element_type=jnp.float32
        )
    update = exact_dot(jnp.transpose(features[...])[0:rows], local_planes[...])
    attended_rows = jnp.concatenate(
        [pair_rows[pl.ds(h, rows, heads), :] for h in range(heads)], axis=1
    )
    update = update + exact_dot(attended_rows, attended[...])
    updated = layer_norm(single[...].astype(jnp.float32) + update, norm_gain[...][None])
    updated = updated.astype(jnp.bfloat16)
    right_own[...] = jnp.dot(
        updated, right_weight[...], preferred_element_type=jnp.float32
    ).astype(jnp.bfloat16)
    start, finish = push_blocks(right_own, right_buf, send_c, recv_c, send_d, recv_d)
    start()
    single_out[...] = updated
    left = jnp.dot(updated, left_weight[...], preferred_element_type=jnp.float32)
    left_out[...] = left.astype(jnp.bfloat16).astype(jnp.float32)

    motion = dot_nt(velocity_weight[...], updated)
    ratio = 1.0 / (STEPS - timestep[0]).astype(jnp.float32)
    live = own[13:14]
    turn_vec = ratio * jnp.tanh(motion[0:3]) * live
    speed = ratio * motion[3:6] * live
    x, y, z = turn_vec[0:1], turn_vec[1:2], turn_vec[2:3]
    angle = x * x + y * y + z * z
    coefs = [jnp.zeros_like(angle)] * 3
    powers = jnp.ones_like(angle)
    for order in range(8):
        parity = (-1.0) ** order
        coefs = [
            coef + powers * (parity / float(math.factorial(2 * order + 1 + i)))
            for i, coef in enumerate(coefs)
        ]
        powers = powers * angle
    zero = jnp.zeros_like(angle)
    cross_mat = [[zero, -z, y], [z, zero, -x], [-y, x, zero]]
    times = lambda p, q: [
        [sum(p[a][b] * q[b][c] for b in range(3)) for c in range(len(q[0]))] for a in range(3)
    ]
    squared = times(cross_mat, cross_mat)
    mix = lambda first, second: [
        [
            (1.0 if a == b else 0.0) + first * cross_mat[a][b] + second * squared[a][b]
            for b in range(3)
        ]
        for a in range(3)
    ]
    turn = mix(coefs[0], coefs[1])
    jacobian = mix(coefs[1], coefs[2])
    own_rot = [[own[3 * a + b : 3 * a + b + 1] for b in range(3)] for a in range(3)]
    new_rot = times(own_rot, turn)
    moved = times(own_rot, times(jacobian, [[speed[a : a + 1]] for a in range(3)]))
    for a in range(3):
        for b in range(3):
            rot_out[a, b : b + 1, :] = new_rot[a][b]
        trans_out[a : a + 1, :] = own[9 + a : 10 + a] + moved[a][0]
    finish()
    right_out[...] = right_buf[...].astype(jnp.float32).reshape(total, right_own.shape[1])


def run_attention(
    single,
    pair,
    rotations,
    translations,
    chain,
    mask,
    timestep,
    proj,
    bias_weight,
    distance_weight,
    chain_offset,
    local,
    attended,
    norm_gain,
    velocity_weight,
    left_weight,
    right_weight,
):
    rows, width = single.shape
    total = rotations.shape[2]
    members = total // rows
    pairs = members // 2
    heads = proj.shape[1]
    channels = pair.shape[2]
    chunks = total // 128
    proj_t = jnp.transpose(proj, (2, 1, 0)).reshape(-1, width)
    local = local.reshape(-1, width)
    attended = attended.reshape(-1, width)
    smem = pl.BlockSpec(memory_space=pltpu.SMEM)
    vmem = pl.BlockSpec(memory_space=pltpu.VMEM)
    hbm = pl.BlockSpec(memory_space=pl.ANY)
    bf16, f32 = jnp.bfloat16, jnp.float32
    shape = jax.ShapeDtypeStruct
    scratch = [
        ((members, rows, width), bf16),
        ((members, rows, channels), bf16),
        ((rows, channels), bf16),
        (pair.shape, bf16),
        (proj_t.shape, bf16),
        (local.shape, bf16),
        (attended.shape, bf16),
        ((16, total), f32),
        ((chunks, proj_t.shape[0], 128), f32),
        ((proj_t.shape[0], 128), f32),
        ((heads * 16, 128), f32),
        ((heads * 3 * PQ, 128), f32),
        ((chunks, heads * ROWS, 128), f32),
        ((heads, total), f32),
        ((chunks, rows * heads, total // chunks), f32),
        ((chunks, rows * heads, total // chunks), f32),
        ((width // 128, heads * 64 + 8, 128), f32),
        ((heads * FEAT, width), bf16),
        ((heads * FEAT, 128), f32),
        ((rows * heads, channels), f32),
    ]
    return pl.pallas_call(
        attention_kernel,
        out_shape=(
            shape((rows, width), bf16),
            shape((3, 3, rows), f32),
            shape((3, rows), f32),
            shape((rows, channels), f32),
            shape((total, channels), f32),
        ),
        in_specs=[smem] * 3 + [vmem] * 10 + [hbm] * 4,
        out_specs=(vmem,) * 5,
        scratch_shapes=[pltpu.VMEM(*item) for item in scratch]
        + [pltpu.SemaphoreType.DMA((4,))]
        + [pltpu.SemaphoreType.DMA((pairs,))] * 8,
        compiler_params=pltpu.CompilerParams(collective_id=2, has_side_effects=True),
        name="attention",
    )(
        timestep,
        distance_weight,
        chain_offset,
        single,
        rotations,
        translations,
        chain,
        mask,
        jnp.transpose(bias_weight),
        norm_gain,
        jnp.transpose(velocity_weight),
        left_weight,
        right_weight,
        pair,
        proj_t,
        local,
        attended,
    )


def shards(
    single,
    pair,
    rotations,
    translations,
    residue_chain_index,
    residue_move_mask,
    timestep,
    single_projection_weight,
    head_bias_weight,
    head_distance_weight,
    chain_logit_offset,
    local_output_weight,
    pair_output_weight,
    single_norm_gain,
    frame_velocity_weight,
    left_pair_weight,
    right_pair_weight,
    pair_norm_gain,
    transition_hidden_weight,
    transition_middle_weight,
    transition_back_weight,
):
    rows_dev = single.shape[0]
    col_count = pair.shape[1]
    total = rotations.shape[2]
    heads_here = single_projection_weight.shape[1]
    row_start = lax.axis_index("res") * rows_dev
    col_start = lax.axis_index("head") * col_count
    if col_count == total:
        single_out, rot_out, trans_out, left_wide, right_wide = run_attention(
            single,
            pair,
            rotations,
            translations,
            residue_chain_index,
            residue_move_mask,
            timestep,
            single_projection_weight,
            head_bias_weight,
            head_distance_weight,
            chain_logit_offset,
            local_output_weight,
            pair_output_weight,
            single_norm_gain,
            frame_velocity_weight,
            left_pair_weight,
            right_pair_weight,
        )
        return run_transition(
            residue_move_mask,
            pair,
            left_wide,
            right_wide,
            residue_move_mask,
            pair_norm_gain,
            transition_hidden_weight,
            transition_middle_weight,
            transition_back_weight,
            single_out,
            rot_out,
            trans_out,
        )
    rot_all = jnp.transpose(rotations, (2, 0, 1))
    trans_all = jnp.transpose(translations)
    rot_own = lax.dynamic_slice_in_dim(rot_all, row_start, rows_dev, 0)
    trans_own = lax.dynamic_slice_in_dim(trans_all, row_start, rows_dev, 0)
    own_chain = lax.dynamic_slice_in_dim(residue_chain_index, row_start, rows_dev, 0)
    offset = 3 * HEAD_FEATURES
    feat_count = 2 * HEAD_FEATURES + 3 * PQ + 3 * PV
    members = total // rows_dev
    every_single = gather_blocks(single, members, 0).reshape(total, -1)
    every_proj = jnp.einsum(
        "nd,dhf->nhf", every_single, single_projection_weight, preferred_element_type=jnp.float32
    )
    projected = lax.dynamic_slice_in_dim(every_proj, row_start, rows_dev, 0)
    packed_projection = key_features(every_proj, rot_all, trans_all)
    packed_projection = packed_projection.reshape(total, heads_here, feat_count)
    query_values = projected[:, :, 0:HEAD_FEATURES].astype(jnp.bfloat16)
    query_flattened = to_global(
        projected[:, :, offset : offset + 3 * PQ], rot_own, trans_own, PQ
    ).reshape(rows_dev, heads_here, 3 * PQ)
    bias_local = jnp.einsum(
        "rjc,ch->rhj", pair, head_bias_weight, preferred_element_type=jnp.float32
    ).astype(jnp.bfloat16)
    pair_head_bias = lax.all_to_all(
        bias_local, "head", split_axis=1, concat_axis=2, tiled=True
    ).astype(jnp.float32)
    within_chain = (own_chain[:, None] == residue_chain_index[None, :]).astype(jnp.float32)
    logit_matrix = local_logit_rows(
        query_values,
        query_flattened,
        packed_projection,
        pair_head_bias,
        within_chain,
        head_distance_weight,
        chain_logit_offset,
        residue_move_mask > 0,
    )
    peak = jnp.max(logit_matrix, axis=-1, keepdims=True)
    exponent = jnp.exp(logit_matrix - peak)
    attention = rounded(exponent / jnp.sum(exponent, axis=-1, keepdims=True))
    scalar_out = jnp.einsum(
        "rhn,nhc->rhc",
        attention,
        packed_projection[:, :, HEAD_FEATURES : 2 * HEAD_FEATURES],
        preferred_element_type=jnp.float32,
    )
    point_global = jnp.einsum(
        "rhn,nhp->rhp",
        attention.astype(jnp.float32),
        packed_projection[:, :, 2 * HEAD_FEATURES + 3 * PQ :].astype(jnp.float32),
        precision=HIGHEST,
    )
    update_local = local_points(scalar_out, point_global, rot_own, trans_own, local_output_weight)
    attention_cols = lax.all_to_all(attention, "head", split_axis=2, concat_axis=1, tiled=True)
    pair_attended = jnp.einsum(
        "rhj,rjc->rhc", attention_cols, pair, preferred_element_type=jnp.float32
    )
    update_pair = jnp.einsum(
        "rhc,hcd->rd", pair_attended, pair_output_weight.astype(jnp.float32), precision=HIGHEST
    )
    update = lax.psum(update_local + update_pair, "head")
    single_out = layer_norm(single.astype(jnp.float32) + update, single_norm_gain).astype(
        jnp.bfloat16
    )
    live_all = (residue_move_mask > 0).astype(jnp.float32)
    live_own = lax.dynamic_slice_in_dim(live_all, row_start, rows_dev, 0)
    step_ratio = 1.0 / (STEPS - timestep[0]).astype(jnp.float32)
    rot_out, trans_out = frame_step(
        single_out, frame_velocity_weight, rot_own, trans_own, live_own, step_ratio
    )
    left_proj = jnp.dot(single_out, left_pair_weight, preferred_element_type=jnp.float32).astype(
        jnp.bfloat16
    )
    own_right = jnp.dot(single_out, right_pair_weight, preferred_element_type=jnp.float32).astype(
        jnp.bfloat16
    )
    every_right = gather_blocks(own_right, members, 1).reshape(total, -1)
    right_proj = lax.dynamic_slice_in_dim(every_right, col_start, col_count, 0)
    (pair_out,) = run_transition(
        residue_move_mask,
        pair,
        left_proj.astype(jnp.float32),
        right_proj.astype(jnp.float32),
        lax.dynamic_slice_in_dim(residue_move_mask, col_start, col_count, 0),
        pair_norm_gain,
        transition_hidden_weight,
        transition_middle_weight,
        transition_back_weight,
    )
    return (single_out, rot_out, trans_out, pair_out)


def solution(mesh):
    placed = (
        P(("batch", "res"), None),
        P(("batch", "res"), "head", None),
        P(None, None, "batch"),
        P(None, "batch"),
        P(),
        P("batch"),
        P(),
        P(None, "head", None),
        P(),
        P("head"),
        P("head"),
        P("head", None, None),
        P(),
        P(),
        P(),
        P(),
        P(),
        P(),
        P(),
        P(),
        P(),
    )
    return jax.shard_map(
        shards,
        mesh=mesh,
        in_specs=placed,
        out_specs=(
            P(("batch", "res"), None),
            P(None, None, ("batch", "res")),
            P(None, ("batch", "res")),
            P(("batch", "res"), "head", None),
        ),
        check_vma=False,
    )
```

profile of v0, /device:TPU:0, one launch (start us, length us, event | category | flops | bytes accessed | tf_op | source)
XLA Modules:
  0.0 35.2 jit_solution(2072421665969998967)
XLA Ops:
  1.3 25.5 %attention.1 = (bf16[24,384]{1,0:T(8,128)(2,1)}, f32[3,3,24]{2,1,0:T(4,128)}, f32[3,24]{1,0:T(4,128)}, f32[24,128]{1,0:T(8,128)}, f32[384,128]{1,0:T(8,128)}) custom-call(s32[1]{0:T(128)S(6)} %copy.25.timestep, f32[16]{0:T(128)} %distance_weight.1, f32[16]{0:T(128)} %chain_offset.1, bf16[24,384]{1,0:T(8,128)(2,1)} %single.1, f32[3,3,384]{2,1,0:T(4,128)} %rotations.1, ...), custom_call_target="tpu_custom_call" | custom-call | tf_op jit(solution)/shard_map/attention/pallas_call | solution.py:646
  26.8 8.4 %transition.1 = (bf16[24,384,128]{2,1,0:T(8,128)(2,1)}, bf16[24,384]{1,0:T(8,128)(2,1)}, f32[3,3,24]{2,1,0:T(4,128)}, f32[3,24]{1,0:T(4,128)}) custom-call(s32[384]{0:T(512)} %live_cols.1, bf16[24,384,128]{2,1,0:T(8,128)(2,1)} %pair.1, f32[24,128]{1,0:T(8,128)} %get-tuple-element.13.left, f32[384,128]{1,0:T(8,128)} %get-tuple-element.14.right, ...), custom_call_target="tpu_custom_call" | custom-call | tf_op jit(solution)/shard_map/transition/pallas_call | solution.py:271
where the time goes:
time: 35.4 us; the launch traced here: 35.2 us
  Pallas kernels  33.9 us (96%)
  between operations  1.29 us (4%)
    pallas_call x1, Pallas kernels, run_attention(): pl.pallas_call(attention_kernel, out_shape=(shape((rows, width), bf16), s...  25.5 us
    pallas_call x1, Pallas kernels, run_transition(): pl.pallas_call(transition_kernel, grid=(rows // block,), out_shape=[jax.S...  8.42 us

commit v1 on v0

--- a/solution.py
+++ b/solution.py
@@ -283,6 +283,8 @@
 
 ROWS = 88
 STACK = 4
+PARTS = 2
+PIECES = 1
 GROUP = 4
 FEAT = 80
 NT = (((1,), (1,)), ((), ()))
@@ -306,10 +308,112 @@
 
 
 def exact_dot(values, weight):
-    return sum(
-        jnp.dot(part, weight, preferred_element_type=jnp.float32)
-        for part in reversed(in_three(values))
-    )
+    rows = values.shape[0]
+    stacked = jnp.concatenate(in_three(values), axis=0)
+    result = jnp.dot(stacked, weight, preferred_element_type=jnp.float32)
+    return result[2 * rows :] + result[rows : 2 * rows] + result[0:rows]
+
+
+def flipped(chip, step):
+    out, bit = chip, 1
+    while bit <= step:
+        if step & bit:
+            out = out + bit * (1 - 2 * lax.rem(chip // bit, 2))
+        bit *= 2
+    return out
+
+
+def position():
+    me = lax.axis_index("res")
+    return me, me // 2, lax.rem(me, 2)
+
+
+def greet_all(count):
+    me, chip, side = position()
+    barrier = pltpu.get_barrier_semaphore()
+    for step in reversed(range(count // 2)):
+        for other in (0, 1):
+            if step or other:
+                target = flipped(chip, step) * 2 + (1 - side if other else side)
+                pl.semaphore_signal(
+                    barrier, inc=1, device_id={"res": target}, device_id_type=pl.DeviceIdType.MESH
+                )
+    return lambda: pl.semaphore_wait(barrier, count - 1)
+
+
+def send_to(src, dst, send_sem, recv_sem, target):
+    return pltpu.make_async_remote_copy(
+        src_ref=src,
+        dst_ref=dst,
+        send_sem=send_sem,
+        recv_sem=recv_sem,
+        device_id={"res": target},
+        device_id_type=pl.DeviceIdType.MESH,
+    )
+
+
+def gather_singles(src, buf, send_a, recv_a, send_b, recv_b):
+    pairs = buf.shape[0] // 2
+    me, chip, side = position()
+    partner = chip * 2 + 1 - side
+
+    def outgoing(step):
+        target = flipped(chip, step) * 2 + side if step else partner
+        return send_to(src, buf.at[me], send_a.at[step], recv_a.at[step], target)
+
+    def passed_on(step):
+        origin = flipped(chip, step) * 2 + side
+        return send_to(buf.at[origin], buf.at[origin], send_b.at[step], recv_b.at[step], partner)
+
+    def start():
+        for step in reversed(range(pairs)):
+            outgoing(step).start()
+        buf[me] = src[...]
+
+    def relay(step):
+        outgoing(step).wait_recv()
+        passed_on(step).start()
+
+    def finish():
+        outgoing(0).wait_recv()
+        for step in range(1, pairs):
+            passed_on(step).wait_recv()
+
+    def drain():
+        for step in range(pairs):
+            outgoing(step).wait_send()
+        for step in range(1, pairs):
+            passed_on(step).wait_send()
+
+    return start, relay, finish, drain
+
+
+def share_block(src, buf, send, recv):
+    pairs = buf.shape[0] // 2
+    me, chip, side = position()
+
+    def outgoing(step, other):
+        target = flipped(chip, step) * 2 + (1 - side if other else side)
+        at = 2 * step + other
+        return send_to(src, buf.at[me], send.at[at], recv.at[at], target)
+
+    everyone = [(step, other) for step in range(pairs) for other in (0, 1) if step or other]
+
+    def start():
+        for step, other in reversed(everyone):
+            outgoing(step, other).start()
+        buf[me] = src[...]
+
+    def arrived(step):
+        for other in (0, 1):
+            if step or other:
+                outgoing(step, other).wait_recv()
+
+    def drain():
+        for step, other in everyone:
+            outgoing(step, other).wait_send()
+
+    return start, arrived, drain
 
 
 def turned_planes(planes, frame, transpose=False):
@@ -324,59 +428,90 @@
     return out
 
 
-def attention_kernel(
-    timestep,
-    distance_weight,
-    chain_offset,
-    single,
-    rotations,
-    translations,
-    chain,
-    mask,
-    bias_weight,
-    norm_gain,
-    velocity_weight,
-    left_weight,
-    right_weight,
-    pair_hbm,
-    proj_hbm,
-    local_hbm,
-    attended_hbm,
-    single_out,
-    rot_out,
-    trans_out,
-    left_out,
-    right_out,
-    buf,
-    right_buf,
-    right_own,
-    pair,
-    proj,
-    local,
-    attended,
-    frames,
-    proj_all,
-    proj_own,
-    query_t,
-    point_t,
-    placed_t,
-    squares,
-    bias,
-    attn,
-    local_wide,
-    local_planes,
-    features,
-    pair_rows,
-    sems,
-    send_a,
-    recv_a,
-    send_b,
-    recv_b,
-    send_c,
-    recv_c,
-    send_d,
-    recv_d,
-):
+OPERANDS = (
+    "distance_weight",
+    "chain_offset",
+    "timestep",
+    "single",
+    "rotations",
+    "translations",
+    "chain",
+    "mask",
+    "bias_weight",
+    "norm_gain",
+    "velocity_weight",
+    "left_weight",
+    "right_weight",
+    "proj",
+    "pair",
+    "local",
+    "attended",
+    "pair_gain",
+    "first",
+    "middle",
+    "back",
+)
+SCALARS = 2
+
+
+def step_kernel(*refs):
+    count = len(OPERANDS)
+    sources, refs = refs[:count], refs[count:]
+    (single_out, rot_out, trans_out, pair_out), refs = refs[:4], refs[4:]
+    held, refs = refs[:count], refs[count:]
+    (
+        buf,
+        right_buf,
+        right_own,
+        frames,
+        proj_all,
+        proj_own,
+        query_t,
+        point_t,
+        placed_t,
+        squares,
+        bias,
+        attn,
+        local_wide,
+        local_planes,
+        features,
+        pair_rows,
+        left_rows,
+        row_gain,
+        live_wide,
+        centred_pair,
+        normed,
+        sems,
+        send_a,
+        recv_a,
+        send_b,
+        recv_b,
+        send_c,
+        recv_c,
+    ) = refs
+    (
+        distance_weight,
+        chain_offset,
+        timestep,
+        single,
+        rotations,
+        translations,
+        chain,
+        mask,
+        bias_weight,
+        norm_gain,
+        velocity_weight,
+        left_weight,
+        right_weight,
+        proj,
+        pair,
+        local,
+        attended,
+        pair_gain,
+        first,
+        middle,
+        back,
+    ) = held
     rows = single.shape[0]
     members = buf.shape[0]
     total = members * rows
@@ -385,18 +520,22 @@
     width = single.shape[1]
     shift = lax.rem(total - lax.axis_index("res") * rows, total)
 
-    loads = [
-        pltpu.make_async_copy(src, dst, sems.at[i])
-        for i, (src, dst) in enumerate(
-            [(proj_hbm, proj), (pair_hbm, pair), (local_hbm, local), (attended_hbm, attended)]
-        )
-    ]
-    for load in loads:
-        load.start()
-    greet(members)
-    start, finish = push_blocks(single, buf, send_a, recv_a, send_b, recv_b)
+    greeted = greet_all(members)
+    loads = {
+        name: pltpu.make_async_copy(src, dst, sems.at[i])
+        for i, (name, src, dst) in enumerate(zip(OPERANDS, sources, held))
+    }
+    order = ["single"] + [name for name in OPERANDS if name != "single"]
+    for name in order:
+        loads[name].start()
+    loads["single"].wait()
+    greeted()
+    start, relay, finish, drain = gather_singles(single, buf, send_a, recv_a, send_b, recv_b)
     start()
 
+    for name in OPERANDS[: OPERANDS.index("proj")]:
+        if name != "single":
+            loads[name].wait()
     for a in range(3):
         frames[3 * a : 3 * a + 3, :] = rotations[a]
     frames[9:12, :] = translations[...]
@@ -409,7 +548,7 @@
     within = jnp.where(own_cols[:, 12:13] == frames[12:13, :], 1.0, 0.0)
     present = jnp.broadcast_to(frames[13:14, :], (rows, total)) > 0
 
-    loads[0].wait()
+    loads["proj"].wait()
     proj_own[:, 0:rows] = dot_nt(proj[...], single[...])
     for h in range(heads):
         query_t[h * 16 : h * 16 + 16, :] = proj_own[pl.ds(h, 16, heads), :]
@@ -427,14 +566,14 @@
             for i in range(4):
                 placed_t[c, pl.ds(at + i, heads, ROWS), :] = jnp.zeros((heads, 128), jnp.float32)
 
-    loads[1].wait()
+    loads["pair"].wait()
     bias_t = bias_weight[...]
     for r in range(rows):
         row = dot_nt(bias_t, pair[r]).astype(jnp.bfloat16).astype(jnp.float32)
         for c in range(chunks):
             bias[c, r * heads : (r + 1) * heads, :] = row[:, c * 128 : (c + 1) * 128]
 
-    loads[2].wait()
+    loads["local"].wait()
     for c in range(width // 128):
         local_wide[c, 0 : heads * 64, :] = local[:, c * 128 : (c + 1) * 128].astype(jnp.float32)
         local_wide[c, heads * 64 : heads * 64 + 8, :] = jnp.zeros((8, 128), jnp.float32)
@@ -449,8 +588,20 @@
             ).astype(jnp.bfloat16)
         plane = lanes(local_wide, base + 52, 16)
         local_planes[at + 64 : at + 80, :] = jnp.where(keep, plane, 0.0).astype(jnp.bfloat16)
-    loads[3].wait()
-
+    for name in OPERANDS[OPERANDS.index("attended") :]:
+        loads[name].wait()
+    live_wide[...] = jnp.transpose(
+        jnp.broadcast_to(frames[13:14, :], (live_wide.shape[1], live_wide.shape[0]))
+    )
+    channels = pair.shape[2]
+    row_gain[...] = own_cols[:, 13:14] * (math.sqrt(channels) * pair_gain[...])[None]
+
+    pairs = members // 2
+    for step in range(1, pairs):
+        for i in range(rows * (step - 1) // (pairs - 1), rows * step // (pairs - 1)):
+            own_pair = pair[i].astype(jnp.float32)
+            centred_pair[i] = own_pair - jnp.mean(own_pair, axis=-1, keepdims=True)
+        relay(step)
     finish()
     every = buf[...].astype(jnp.float32).reshape(total, width).astype(jnp.bfloat16)
     for c in range(chunks):
@@ -539,14 +690,15 @@
     right_own[...] = jnp.dot(
         updated, right_weight[...], preferred_element_type=jnp.float32
     ).astype(jnp.bfloat16)
-    start, finish = push_blocks(right_own, right_buf, send_c, recv_c, send_d, recv_d)
-    start()
+    share, arrived, settle = share_block(right_own, right_buf, send_c, recv_c)
+    share()
     single_out[...] = updated
     left = jnp.dot(updated, left_weight[...], preferred_element_type=jnp.float32)
-    left_out[...] = left.astype(jnp.bfloat16).astype(jnp.float32)
+    left = left.astype(jnp.bfloat16).astype(jnp.float32)
+    left_rows[...] = left - jnp.mean(left, axis=-1, keepdims=True)
 
     motion = dot_nt(velocity_weight[...], updated)
-    ratio = 1.0 / (STEPS - timestep[0]).astype(jnp.float32)
+    ratio = 1.0 / (STEPS - timestep[...]).astype(jnp.float32)
     live = own[13:14]
     turn_vec = ratio * jnp.tanh(motion[0:3]) * live
     speed = ratio * motion[3:6] * live
@@ -583,11 +735,82 @@
         for b in range(3):
             rot_out[a, b : b + 1, :] = new_rot[a][b]
         trans_out[a : a + 1, :] = own[9 + a : 10 + a] + moved[a][0]
-    finish()
-    right_out[...] = right_buf[...].astype(jnp.float32).reshape(total, right_own.shape[1])
-
-
-def run_attention(
+    drain()
+
+    chip = position()[1]
+    span = 2 * rows
+
+    def columns(step):
+        return pl.ds(pl.multiple_of(flipped(chip, step) * span, span), span)
+
+    def prepare(step):
+        at = columns(step)
+        q = flipped(chip, step)
+        arrived(step)
+        right = jnp.concatenate([right_buf[2 * q], right_buf[2 * q + 1]], axis=0)
+        right = right.astype(jnp.float32)
+        right = right - jnp.mean(right, axis=-1, keepdims=True)
+        live = live_wide[at, :]
+        for i in range(rows):
+            centred = centred_pair[i, at, :] + (left_rows[i : i + 1, :] + right)
+            spread = jnp.sum(centred * centred, axis=-1, keepdims=True) + channels * 1e-05
+            scaled = centred * (lax.rsqrt(spread) * live) * row_gain[i : i + 1, :]
+            normed[step % 2, i * span : (i + 1) * span, :] = scaled.astype(jnp.bfloat16)
+
+    def apply(step):
+        at = columns(step)
+        part = rows // PARTS
+        for top in range(0, rows, part):
+            hidden = normed[step % 2, top * span : (top + part) * span, :]
+            hidden = jnp.dot(hidden, first[...], preferred_element_type=jnp.float32)
+            hidden = jnp.maximum(hidden.astype(jnp.bfloat16), 0)
+            hidden = jnp.dot(hidden, middle[...], preferred_element_type=jnp.float32)
+            hidden = jnp.maximum(hidden.astype(jnp.bfloat16), 0)
+            branch = jnp.dot(hidden, back[...], preferred_element_type=jnp.float32)
+            for i in range(top, top + part):
+                added = branch[(i - top) * span : (i - top + 1) * span]
+                own_pair = pair[i, at, :].astype(jnp.float32)
+                pair_out[i, at, :] = (own_pair + added).astype(jnp.bfloat16)
+
+    steps = members // 2
+    prepare(0)
+    for step in range(steps):
+        if step + 1 < steps:
+            prepare(step + 1)
+        apply(step)
+    settle()
+
+
+def deliver_kernel(*refs):
+    *refs, sems = refs
+    half = len(refs) // 2
+    parts = []
+    for src, dst in zip(refs[:half], refs[half:]):
+        rows = src.shape[0]
+        piece = rows // PIECES if len(src.shape) == 3 and rows % PIECES == 0 else rows
+        for top in range(0, rows, piece):
+            parts.append((src.at[pl.ds(top, piece)], dst.at[pl.ds(top, piece)]))
+    copies = [
+        pltpu.make_async_copy(src, dst, sems.at[i]) for i, (src, dst) in enumerate(parts)
+    ]
+    for copy in reversed(copies):
+        copy.start()
+    for copy in copies:
+        copy.wait()
+
+
+def deliver(*arrays):
+    return pl.pallas_call(
+        deliver_kernel,
+        out_shape=[jax.ShapeDtypeStruct(a.shape, a.dtype) for a in arrays],
+        in_specs=[pl.BlockSpec(memory_space=pltpu.VMEM)] * len(arrays),
+        out_specs=[pl.BlockSpec(memory_space=pl.ANY)] * len(arrays),
+        scratch_shapes=[pltpu.SemaphoreType.DMA((len(arrays) * PIECES,))],
+        name="deliver",
+    )(*[pltpu.with_memory_space_constraint(a, pltpu.VMEM) for a in arrays])
+
+
+def run_step(
     single,
     pair,
     rotations,
@@ -605,6 +828,10 @@
     velocity_weight,
     left_weight,
     right_weight,
+    pair_gain,
+    first,
+    middle,
+    back,
 ):
     rows, width = single.shape
     total = rotations.shape[2]
@@ -614,21 +841,35 @@
     channels = pair.shape[2]
     chunks = total // 128
     proj_t = jnp.transpose(proj, (2, 1, 0)).reshape(-1, width)
-    local = local.reshape(-1, width)
-    attended = attended.reshape(-1, width)
-    smem = pl.BlockSpec(memory_space=pltpu.SMEM)
-    vmem = pl.BlockSpec(memory_space=pltpu.VMEM)
-    hbm = pl.BlockSpec(memory_space=pl.ANY)
+    operands = dict(
+        timestep=timestep.reshape(1, 1),
+        distance_weight=distance_weight,
+        chain_offset=chain_offset,
+        single=single,
+        rotations=rotations,
+        translations=translations,
+        chain=chain,
+        mask=mask,
+        bias_weight=jnp.transpose(bias_weight),
+        norm_gain=norm_gain,
+        velocity_weight=jnp.transpose(velocity_weight),
+        left_weight=left_weight,
+        right_weight=right_weight,
+        proj=proj_t,
+        pair=pair,
+        local=local.reshape(-1, width),
+        attended=attended.reshape(-1, width),
+        pair_gain=pair_gain,
+        first=first,
+        middle=middle,
+        back=back,
+    )
+    operands = [operands[name] for name in OPERANDS]
     bf16, f32 = jnp.bfloat16, jnp.float32
-    shape = jax.ShapeDtypeStruct
     scratch = [
         ((members, rows, width), bf16),
         ((members, rows, channels), bf16),
         ((rows, channels), bf16),
-        (pair.shape, bf16),
-        (proj_t.shape, bf16),
-        (local.shape, bf16),
-        (attended.shape, bf16),
         ((16, total), f32),
         ((chunks, proj_t.shape[0], 128), f32),
         ((proj_t.shape[0], 128), f32),
@@ -642,42 +883,33 @@
         ((heads * FEAT, width), bf16),
         ((heads * FEAT, 128), f32),
         ((rows * heads, channels), f32),
+        ((rows, channels), f32),
+        ((rows, channels), f32),
+        ((total, channels), f32),
+        (pair.shape, f32),
+        ((2, 2 * rows * rows, channels), bf16),
     ]
-    return pl.pallas_call(
-        attention_kernel,
+    dma = pltpu.SemaphoreType.DMA
+    results = pl.pallas_call(
+        step_kernel,
         out_shape=(
-            shape((rows, width), bf16),
-            shape((3, 3, rows), f32),
-            shape((3, rows), f32),
-            shape((rows, channels), f32),
-            shape((total, channels), f32),
+            pltpu.VMEM((rows, width), bf16),
+            pltpu.VMEM((3, 3, rows), f32),
+            pltpu.VMEM((3, rows), f32),
+            pltpu.VMEM(pair.shape, bf16),
         ),
-        in_specs=[smem] * 3 + [vmem] * 10 + [hbm] * 4,
-        out_specs=(vmem,) * 5,
-        scratch_shapes=[pltpu.VMEM(*item) for item in scratch]
-        + [pltpu.SemaphoreType.DMA((4,))]
-        + [pltpu.SemaphoreType.DMA((pairs,))] * 8,
+        in_specs=[pl.BlockSpec(memory_space=pl.ANY)] * len(operands),
+        out_specs=(pl.BlockSpec(memory_space=pltpu.VMEM),) * 4,
+        scratch_shapes=[pltpu.SMEM(a.shape, a.dtype) for a in operands[:SCALARS]]
+        + [pltpu.VMEM(a.shape, a.dtype) for a in operands[SCALARS:]]
+        + [pltpu.VMEM(*item) for item in scratch]
+        + [dma((len(operands),))]
+        + [dma((pairs,))] * 4
+        + [dma((members,))] * 2,
         compiler_params=pltpu.CompilerParams(collective_id=2, has_side_effects=True),
-        name="attention",
-    )(
-        timestep,
-        distance_weight,
-        chain_offset,
-        single,
-        rotations,
-        translations,
-        chain,
-        mask,
-        jnp.transpose(bias_weight),
-        norm_gain,
-        jnp.transpose(velocity_weight),
-        left_weight,
-        right_weight,
-        pair,
-        proj_t,
-        local,
-        attended,
-    )
+        name="step",
+    )(*operands)
+    return deliver(*results)
 
 
 def shards(
@@ -709,39 +941,32 @@
     heads_here = single_projection_weight.shape[1]
     row_start = lax.axis_index("res") * rows_dev
     col_start = lax.axis_index("head") * col_count
-    if col_count == total:
-        single_out, rot_out, trans_out, left_wide, right_wide = run_attention(
-            single,
-            pair,
-            rotations,
-            translations,
-            residue_chain_index,
-            residue_move_mask,
-            timestep,
-            single_projection_weight,
-            head_bias_weight,
-            head_distance_weight,
-            chain_logit_offset,
-            local_output_weight,
-            pair_output_weight,
-            single_norm_gain,
-            frame_velocity_weight,
-            left_pair_weight,
-            right_pair_weight,
-        )
-        return run_transition(
-            residue_move_mask,
-            pair,
-            left_wide,
-            right_wide,
-            residue_move_mask,
-            pair_norm_gain,
-            transition_hidden_weight,
-            transition_middle_weight,
-            transition_back_weight,
-            single_out,
-            rot_out,
-            trans_out,
+    pairs = total // rows_dev // 2
+    if col_count == total and pairs & (pairs - 1) == 0 and rows_dev % 8 == 0:
+        return tuple(
+            run_step(
+                single,
+                pair,
+                rotations,
+                translations,
+                residue_chain_index,
+                residue_move_mask,
+                timestep,
+                single_projection_weight,
+                head_bias_weight,
+                head_distance_weight,
+                chain_logit_offset,
+                local_output_weight,
+                pair_output_weight,
+                single_norm_gain,
+                frame_velocity_weight,
+                left_pair_weight,
+                right_pair_weight,
+                pair_norm_gain,
+                transition_hidden_weight,
+                transition_middle_weight,
+                transition_back_weight,
+            )
         )
     rot_all = jnp.transpose(rotations, (2, 0, 1))
     trans_all = jnp.transpose(translations)

time: 35.4 us -> 29.8 us (0.84)
  Pallas kernels: 33.9 us -> 28.4 us
    pallas_call x2, Pallas kernels: 33.9 us -> 28.4 us  [the longest x1 26.9 us: run_step(): pl.pallas_call(step_kernel, out_shape=(pltpu.VMEM((rows, width), bf16), p...]
where the time goes in v1:
time: 29.8 us; the launch traced here: 29.7 us
  Pallas kernels  28.4 us (95%)
  between operations  1.29 us (4%)
    pallas_call x1, Pallas kernels, run_step(): pl.pallas_call(step_kernel, out_shape=(pltpu.VMEM((rows, width), bf16), p...  26.9 us
    pallas_call x1, Pallas kernels, deliver(): pl.pallas_call(deliver_kernel, out_shape=[jax.ShapeDtypeStruct(a.shape, a...  1.44 us

profile of v1, /device:TPU:0, one launch (start us, length us, event | category | flops | bytes accessed | tf_op | source)
XLA Modules:
  0.0 29.7 jit_solution(12446127424983115341)
XLA Ops:
  1.3 26.9 %step.1 = (bf16[24,384]{1,0:T(8,128)(2,1)S(1)}, f32[3,3,24]{2,1,0:T(4,128)S(1)}, f32[3,24]{1,0:T(4,128)S(1)}, bf16[24,384,128]{2,1,0:T(8,128)(2,1)S(1)}) custom-call(f32[16]{0:T(128)} %refs_0_.1, f32[16]{0:T(128)} %refs_1_.1, s32[1,1]{1,0:T(1,128)} %bitcast.8.refs_2_, bf16[24,384]{1,0:T(8,128)(2,1)} %refs_3_.1, f32[3,3,384]{2,1,0:T(4,128)} %refs_4_.1, ...), custom_call_target="tpu_custom_call" | custom-call | tf_op jit(solution)/shard_map/step/pallas_call | solution.py:893
  28.2 1.4 %deliver.1 = (bf16[24,384]{1,0:T(8,128)(2,1)}, f32[3,3,24]{2,1,0:T(4,128)}, f32[3,24]{1,0:T(4,128)}, bf16[24,384,128]{2,1,0:T(8,128)(2,1)}) custom-call(bf16[24,384]{1,0:T(8,128)(2,1)S(1)} %get-tuple-element.8.refs_0_, f32[3,3,24]{2,1,0:T(4,128)S(1)} %get-tuple-element.9.refs_1_, f32[3,24]{1,0:T(4,128)S(1)} %get-tuple-element.10.refs_2_, ...), custom_call_target="tpu_custom_call" | custom-call | tf_op jit(solution)/shard_map/deliver/pallas_call | solution.py:803

commit v2 on v1

--- a/solution.py
+++ b/solution.py
@@ -284,7 +284,7 @@
 ROWS = 88
 STACK = 4
 PARTS = 2
-PIECES = 1
+LATE = 2
 GROUP = 4
 FEAT = 80
 NT = (((1,), (1,)), ((), ()))
@@ -321,6 +321,10 @@
             out = out + bit * (1 - 2 * lax.rem(chip // bit, 2))
         bit *= 2
     return out
+
+
+def chip_columns(chip, step, span):
+    return pl.ds(pl.multiple_of(flipped(chip, step) * span, span), span)
 
 
 def position():
@@ -354,30 +358,31 @@
 
 def gather_singles(src, buf, send_a, recv_a, send_b, recv_b):
     pairs = buf.shape[0] // 2
-    me, chip, side = position()
+    _, chip, side = position()
     partner = chip * 2 + 1 - side
 
     def outgoing(step):
         target = flipped(chip, step) * 2 + side if step else partner
-        return send_to(src, buf.at[me], send_a.at[step], recv_a.at[step], target)
+        return send_to(src, buf.at[2 * step + side], send_a.at[step], recv_a.at[step], target)
 
     def passed_on(step):
-        origin = flipped(chip, step) * 2 + side
-        return send_to(buf.at[origin], buf.at[origin], send_b.at[step], recv_b.at[step], partner)
+        block = buf.at[2 * step + side]
+        return send_to(block, block, send_b.at[step], recv_b.at[step], partner)
 
     def start():
         for step in reversed(range(pairs)):
             outgoing(step).start()
-        buf[me] = src[...]
+        buf[side] = src[...]
 
     def relay(step):
         outgoing(step).wait_recv()
         passed_on(step).start()
 
-    def finish():
-        outgoing(0).wait_recv()
-        for step in range(1, pairs):
+    def complete(step):
+        if step:
             passed_on(step).wait_recv()
+        else:
+            outgoing(0).wait_recv()
 
     def drain():
         for step in range(pairs):
@@ -385,24 +390,24 @@
         for step in range(1, pairs):
             passed_on(step).wait_send()
 
-    return start, relay, finish, drain
+    return start, relay, complete, drain
 
 
 def share_block(src, buf, send, recv):
     pairs = buf.shape[0] // 2
-    me, chip, side = position()
+    _, chip, side = position()
 
     def outgoing(step, other):
         target = flipped(chip, step) * 2 + (1 - side if other else side)
         at = 2 * step + other
-        return send_to(src, buf.at[me], send.at[at], recv.at[at], target)
+        return send_to(src, buf.at[2 * step + side], send.at[at], recv.at[at], target)
 
     everyone = [(step, other) for step in range(pairs) for other in (0, 1) if step or other]
 
     def start():
-        for step, other in reversed(everyone):
+        for step, other in everyone:
             outgoing(step, other).start()
-        buf[me] = src[...]
+        buf[side] = src[...]
 
     def arrived(step):
         for other in (0, 1):
@@ -457,13 +462,15 @@
 def step_kernel(*refs):
     count = len(OPERANDS)
     sources, refs = refs[:count], refs[count:]
-    (single_out, rot_out, trans_out, pair_out), refs = refs[:4], refs[4:]
-    held, refs = refs[:count], refs[count:]
+    single_out, rot_out, trans_out, pair_out, left_over, *weights_out = refs[:8]
+    refs = refs[8:]
+    held, refs = refs[: count - 3] + tuple(weights_out), refs[count - 3 :]
     (
         buf,
         right_buf,
         right_own,
         frames,
+        frames_t,
         proj_all,
         proj_own,
         query_t,
@@ -482,6 +489,7 @@
         centred_pair,
         normed,
         sems,
+        pair_sems,
         send_a,
         recv_a,
         send_b,
@@ -518,19 +526,34 @@
     heads = bias_weight.shape[0]
     chunks = total // 128
     width = single.shape[1]
-    shift = lax.rem(total - lax.axis_index("res") * rows, total)
+    pairs = members // 2
+    span = 2 * rows
+    me, chip, side = position()
+    shift = lax.rem(total - side * rows, total)
 
     greeted = greet_all(members)
     loads = {
         name: pltpu.make_async_copy(src, dst, sems.at[i])
         for i, (name, src, dst) in enumerate(zip(OPERANDS, sources, held))
+        if name != "pair"
     }
-    order = ["single"] + [name for name in OPERANDS if name != "single"]
-    for name in order:
-        loads[name].start()
+    loads["single"].start()
+    for name, load in loads.items():
+        if name != "single":
+            load.start()
+    pair_loads = [
+        pltpu.make_async_copy(
+            sources[OPERANDS.index("pair")].at[:, chip_columns(chip, step, span), :],
+            pair.at[:, pl.ds(step * span, span), :],
+            pair_sems.at[step],
+        )
+        for step in range(pairs)
+    ]
+    for load in pair_loads:
+        load.start()
     loads["single"].wait()
     greeted()
-    start, relay, finish, drain = gather_singles(single, buf, send_a, recv_a, send_b, recv_b)
+    start, relay, complete, drain = gather_singles(single, buf, send_a, recv_a, send_b, recv_b)
     start()
 
     for name in OPERANDS[: OPERANDS.index("proj")]:
@@ -542,9 +565,16 @@
     frames[12:13, :] = chain[...].astype(jnp.float32)[None]
     frames[13:14, :] = jnp.where(mask[...] > 0, 1.0, 0.0)[None]
     frames[14:16, :] = jnp.zeros((2, total), jnp.float32)
-    own_wide = pltpu.roll(frames[...], shift, 1)[:, 0:128]
+    frames_t[...] = jnp.transpose(frames[...])
+    own_cols = frames_t[pl.ds(pl.multiple_of(me * rows, rows), rows), :]
+    near_t = jnp.concatenate(
+        [frames_t[chip_columns(chip, step, span), :] for step in range(pairs)], axis=0
+    )
+    live_wide[...] = jnp.broadcast_to(near_t[:, 13:14], live_wide.shape)
+    frame = jnp.transpose(near_t)
+    frames[...] = frame
+    own_wide = pltpu.roll(frame, shift, 1)[:, 0:128]
     own = own_wide[:, 0:rows]
-    own_cols = jnp.transpose(own_wide)[0:rows]
     within = jnp.where(own_cols[:, 12:13] == frames[12:13, :], 1.0, 0.0)
     present = jnp.broadcast_to(frames[13:14, :], (rows, total)) > 0
 
@@ -566,7 +596,8 @@
             for i in range(4):
                 placed_t[c, pl.ds(at + i, heads, ROWS), :] = jnp.zeros((heads, 128), jnp.float32)
 
-    loads["pair"].wait()
+    for load in pair_loads:
+        load.wait()
     bias_t = bias_weight[...]
     for r in range(rows):
         row = dot_nt(bias_t, pair[r]).astype(jnp.bfloat16).astype(jnp.float32)
@@ -590,38 +621,50 @@
         local_planes[at + 64 : at + 80, :] = jnp.where(keep, plane, 0.0).astype(jnp.bfloat16)
     for name in OPERANDS[OPERANDS.index("attended") :]:
         loads[name].wait()
-    live_wide[...] = jnp.transpose(
-        jnp.broadcast_to(frames[13:14, :], (live_wide.shape[1], live_wide.shape[0]))
-    )
     channels = pair.shape[2]
     row_gain[...] = own_cols[:, 13:14] * (math.sqrt(channels) * pair_gain[...])[None]
 
-    pairs = members // 2
-    for step in range(1, pairs):
-        for i in range(rows * (step - 1) // (pairs - 1), rows * step // (pairs - 1)):
+    def centre(top, bottom):
+        for i in range(top, bottom):
             own_pair = pair[i].astype(jnp.float32)
             centred_pair[i] = own_pair - jnp.mean(own_pair, axis=-1, keepdims=True)
+
+    def project(c):
+        lead = c * 128 // rows
+        blocks = [buf[m].astype(jnp.float32) for m in range(lead, -(-(c + 1) * 128 // rows))]
+        skip = c * 128 - lead * rows
+        every = jnp.concatenate(blocks, axis=0)[skip : skip + 128]
+        proj_all[c] = dot_nt(proj[...], every.astype(jnp.bfloat16))
+        at_lanes = slice(c * 128, (c + 1) * 128)
+        turn_here = frames[:, at_lanes]
+        key_square = jnp.zeros((heads, 128), jnp.float32)
+        for p in range(PQ + PV):
+            at = 72 + 3 * p
+            planes = [proj_all[c, (at + k) * heads : (at + k + 1) * heads, :] for k in range(3)]
+            for k, plane in enumerate(turned_planes(planes, turn_here)):
+                plane = plane + turn_here[9 + k : 10 + k]
+                plane = plane.astype(jnp.bfloat16).astype(jnp.float32)
+                if p < PQ:
+                    key_square = key_square + plane * plane
+                    slot = 3 * p + k
+                else:
+                    slot = 24 + 16 * k + p - PQ
+                placed_t[c, pl.ds(slot, heads, ROWS), :] = plane
+        squares[:, at_lanes] = key_square
+
+    half = pairs // 2
+    for step in range(1, half):
         relay(step)
-    finish()
-    every = buf[...].astype(jnp.float32).reshape(total, width).astype(jnp.bfloat16)
+    centre(0, rows)
+    for step in range(half, pairs):
+        relay(step)
+    known = 0
     for c in range(chunks):
-        proj_all[c] = dot_nt(proj[...], every[c * 128 : (c + 1) * 128])
-
-    frame = frames[...]
-    key_square = jnp.zeros((heads, total), jnp.float32)
-    for p in range(PQ + PV):
-        at = 72 + 3 * p
-        planes = [lanes(proj_all, (at + c) * heads, heads) for c in range(3)]
-        for c, plane in enumerate(turned_planes(planes, frame)):
-            plane = (plane + frame[9 + c : 10 + c]).astype(jnp.bfloat16).astype(jnp.float32)
-            if p < PQ:
-                key_square = key_square + plane * plane
-                slot = 3 * p + c
-            else:
-                slot = 24 + 16 * c + p - PQ
-            for k in range(chunks):
-                placed_t[k, pl.ds(slot, heads, ROWS), :] = plane[:, k * 128 : (k + 1) * 128]
-    squares[...] = key_square
+        need = min(pairs - 1, ((c + 1) * 128 - 1) // span)
+        for step in range(known, need + 1):
+            complete(step)
+        known = need + 1
+        project(c)
 
     for group in range(0, heads, GROUP):
         members_here = range(group, group + GROUP)
@@ -737,75 +780,108 @@
         trans_out[a : a + 1, :] = own[9 + a : 10 + a] + moved[a][0]
     drain()
 
-    chip = position()[1]
-    span = 2 * rows
-
-    def columns(step):
-        return pl.ds(pl.multiple_of(flipped(chip, step) * span, span), span)
-
     def prepare(step):
-        at = columns(step)
-        q = flipped(chip, step)
+        at = pl.ds(step * span, span)
         arrived(step)
-        right = jnp.concatenate([right_buf[2 * q], right_buf[2 * q + 1]], axis=0)
+        right = jnp.concatenate([right_buf[2 * step], right_buf[2 * step + 1]], axis=0)
         right = right.astype(jnp.float32)
         right = right - jnp.mean(right, axis=-1, keepdims=True)
         live = live_wide[at, :]
+        late = step - (pairs - LATE)
+        into = normed.at[step % 2] if late < 0 else left_over.at[late]
         for i in range(rows):
             centred = centred_pair[i, at, :] + (left_rows[i : i + 1, :] + right)
             spread = jnp.sum(centred * centred, axis=-1, keepdims=True) + channels * 1e-05
             scaled = centred * (lax.rsqrt(spread) * live) * row_gain[i : i + 1, :]
-            normed[step % 2, i * span : (i + 1) * span, :] = scaled.astype(jnp.bfloat16)
-
-    def apply(step):
-        at = columns(step)
-        part = rows // PARTS
-        for top in range(0, rows, part):
-            hidden = normed[step % 2, top * span : (top + part) * span, :]
-            hidden = jnp.dot(hidden, first[...], preferred_element_type=jnp.float32)
-            hidden = jnp.maximum(hidden.astype(jnp.bfloat16), 0)
-            hidden = jnp.dot(hidden, middle[...], preferred_element_type=jnp.float32)
-            hidden = jnp.maximum(hidden.astype(jnp.bfloat16), 0)
-            branch = jnp.dot(hidden, back[...], preferred_element_type=jnp.float32)
-            for i in range(top, top + part):
-                added = branch[(i - top) * span : (i - top + 1) * span]
-                own_pair = pair[i, at, :].astype(jnp.float32)
-                pair_out[i, at, :] = (own_pair + added).astype(jnp.bfloat16)
-
-    steps = members // 2
+            into[i * span : (i + 1) * span, :] = scaled.astype(jnp.bfloat16)
+        if late >= 0:
+            pair_out[:, at, :] = pair[:, at, :]
+
     prepare(0)
-    for step in range(steps):
-        if step + 1 < steps:
-            prepare(step + 1)
-        apply(step)
+    for step in range(pairs - LATE):
+        prepare(step + 1)
+        if step + 1 == pairs - LATE:
+            for late in range(step + 2, pairs):
+                prepare(late)
+        at = step * span
+        add_branch(normed.at[step % 2], pair, pair_out, at, span, first, middle, back)
     settle()
 
 
-def deliver_kernel(*refs):
-    *refs, sems = refs
-    half = len(refs) // 2
-    parts = []
-    for src, dst in zip(refs[:half], refs[half:]):
-        rows = src.shape[0]
-        piece = rows // PIECES if len(src.shape) == 3 and rows % PIECES == 0 else rows
-        for top in range(0, rows, piece):
-            parts.append((src.at[pl.ds(top, piece)], dst.at[pl.ds(top, piece)]))
-    copies = [
-        pltpu.make_async_copy(src, dst, sems.at[i]) for i, (src, dst) in enumerate(parts)
+def add_branch(normed, pair, out, at, span, first, middle, back, out_at=None):
+    rows = pair.shape[0]
+    part = rows // PARTS
+    out_at = at if out_at is None else out_at
+    for top in range(0, rows, part):
+        hidden = normed[top * span : (top + part) * span, :]
+        hidden = jnp.dot(hidden, first[...], preferred_element_type=jnp.float32)
+        hidden = jnp.maximum(hidden.astype(jnp.bfloat16), 0)
+        hidden = jnp.dot(hidden, middle[...], preferred_element_type=jnp.float32)
+        hidden = jnp.maximum(hidden.astype(jnp.bfloat16), 0)
+        branch = jnp.dot(hidden, back[...], preferred_element_type=jnp.float32)
+        for i in range(top, top + part):
+            added = branch[(i - top) * span : (i - top + 1) * span]
+            own_pair = pair[i, pl.ds(at, span), :].astype(jnp.float32)
+            out[i, pl.ds(out_at, span), :] = (own_pair + added).astype(jnp.bfloat16)
+
+
+def deliver_kernel(
+    single,
+    rot,
+    trans,
+    pair,
+    left_over,
+    first,
+    middle,
+    back,
+    single_out,
+    rot_out,
+    trans_out,
+    pair_out,
+    block,
+    sems,
+):
+    _, chip, _ = position()
+    span = 2 * pair.shape[0]
+    pairs = pair.shape[1] // span
+
+    def place(src, step):
+        return pltpu.make_async_copy(
+            src, pair_out.at[:, chip_columns(chip, step, span), :], sems.at[step]
+        )
+
+    copies = [place(pair.at[:, pl.ds(s * span, span), :], s) for s in range(pairs - LATE)]
+    copies += [
+        pltpu.make_async_copy(src, dst, sems.at[pairs + i])
+        for i, (src, dst) in enumerate(
+            [(single, single_out), (rot, rot_out), (trans, trans_out)]
+        )
     ]
-    for copy in reversed(copies):
+    for copy in copies:
         copy.start()
+    for late in range(LATE):
+        step = pairs - LATE + late
+        into = block.at[late]
+        add_branch(left_over.at[late], pair, into, step * span, span, first, middle, back, 0)
+        last = place(into, step)
+        last.start()
+        copies.append(last)
     for copy in copies:
         copy.wait()
 
 
 def deliver(*arrays):
+    rows, cols, channels = arrays[3].shape
+    pairs = cols // (2 * rows)
     return pl.pallas_call(
         deliver_kernel,
-        out_shape=[jax.ShapeDtypeStruct(a.shape, a.dtype) for a in arrays],
+        out_shape=[jax.ShapeDtypeStruct(a.shape, a.dtype) for a in arrays[:4]],
         in_specs=[pl.BlockSpec(memory_space=pltpu.VMEM)] * len(arrays),
-        out_specs=[pl.BlockSpec(memory_space=pl.ANY)] * len(arrays),
-        scratch_shapes=[pltpu.SemaphoreType.DMA((len(arrays) * PIECES,))],
+        out_specs=[pl.BlockSpec(memory_space=pl.ANY)] * 4,
+        scratch_shapes=[
+            pltpu.VMEM((LATE, rows, 2 * rows, channels), arrays[3].dtype),
+            pltpu.SemaphoreType.DMA((pairs + 3,)),
+        ],
         name="deliver",
     )(*[pltpu.with_memory_space_constraint(a, pltpu.VMEM) for a in arrays])
 
@@ -871,6 +947,7 @@
         ((members, rows, channels), bf16),
         ((rows, channels), bf16),
         ((16, total), f32),
+        ((total, 16), f32),
         ((chunks, proj_t.shape[0], 128), f32),
         ((proj_t.shape[0], 128), f32),
         ((heads * 16, 128), f32),
@@ -897,13 +974,15 @@
             pltpu.VMEM((3, 3, rows), f32),
             pltpu.VMEM((3, rows), f32),
             pltpu.VMEM(pair.shape, bf16),
+            pltpu.VMEM((LATE, 2 * rows * rows, channels), bf16),
+            *[pltpu.VMEM(a.shape, a.dtype) for a in operands[-3:]],
         ),
         in_specs=[pl.BlockSpec(memory_space=pl.ANY)] * len(operands),
-        out_specs=(pl.BlockSpec(memory_space=pltpu.VMEM),) * 4,
+        out_specs=(pl.BlockSpec(memory_space=pltpu.VMEM),) * 8,
         scratch_shapes=[pltpu.SMEM(a.shape, a.dtype) for a in operands[:SCALARS]]
-        + [pltpu.VMEM(a.shape, a.dtype) for a in operands[SCALARS:]]
+        + [pltpu.VMEM(a.shape, a.dtype) for a in operands[SCALARS:-3]]
         + [pltpu.VMEM(*item) for item in scratch]
-        + [dma((len(operands),))]
+        + [dma((len(operands),)), dma((pairs,))]
         + [dma((pairs,))] * 4
         + [dma((members,))] * 2,
         compiler_params=pltpu.CompilerParams(collective_id=2, has_side_effects=True),
@@ -942,7 +1021,7 @@
     row_start = lax.axis_index("res") * rows_dev
     col_start = lax.axis_index("head") * col_count
     pairs = total // rows_dev // 2
-    if col_count == total and pairs & (pairs - 1) == 0 and rows_dev % 8 == 0:
+    if col_count == total and pairs & (pairs - 1) == 0 and pairs > LATE and rows_dev % 8 == 0:
         return tuple(
             run_step(
                 single,

time: 29.8 us -> 28.9 us (0.970)
  Pallas kernels: 28.4 us -> 27.5 us
    pallas_call x1, Pallas kernels: 26.9 us -> 25.2 us  [run_step(): pl.pallas_call(step_kernel, out_shape=(pltpu.VMEM((rows, width), bf16), p...]
    pallas_call x1, Pallas kernels: 1.44 us -> 2.27 us  [deliver(): pl.pallas_call(deliver_kernel, out_shape=[jax.ShapeDtypeStruct(a.shape, a...]
where the time goes in v2:
time: 28.9 us; the launch traced here: 28.8 us
  Pallas kernels  27.5 us (95%)
  between operations  1.29 us (4%)
    pallas_call x1, Pallas kernels, run_step(): pl.pallas_call(step_kernel, out_shape=(pltpu.VMEM((rows, width), bf16), p...  25.2 us
    pallas_call x1, Pallas kernels, deliver(): pl.pallas_call(deliver_kernel, out_shape=[jax.ShapeDtypeStruct(a.shape, a...  2.27 us

profile of v2, /device:TPU:0, one launch (start us, length us, event | category | flops | bytes accessed | tf_op | source)
XLA Modules:
  0.0 28.8 jit_solution(5618398140999578030)
XLA Ops:
  1.3 25.2 %step.1 = (bf16[24,384]{1,0:T(8,128)(2,1)S(1)}, f32[3,3,24]{2,1,0:T(4,128)S(1)}, f32[3,24]{1,0:T(4,128)S(1)}, bf16[24,384,128]{2,1,0:T(8,128)(2,1)S(1)}, bf16[2,...) custom-call(f32[16]{0:T(128)} %refs_0_.1, ...), custom_call_target="tpu_custom_call" | custom-call | tf_op jit(solution)/shard_map/step/pallas_call | solution.py:970
  26.5 2.3 %deliver.1 = (bf16[24,384]{1,0:T(8,128)(2,1)}, f32[3,3,24]{2,1,0:T(4,128)}, f32[3,24]{1,0:T(4,128)}, bf16[24,384,128]{2,1,0:T(8,128)(2,1)}) custom-call(bf16[24,384]{1,0:T(8,128)(2,1)S(1)} %get-tuple-element.12.single, f32[3,3,24]{2,1,0:T(4,128)S(1)} %get-tuple-element.13.rot, f32[3,24]{1,0:T(4,128)S(1)} %get-tuple-element.14.trans, ...), custom_call_target="tpu_custom_call" | custom-call | tf_op jit(solution)/shard_map/deliver/pallas_call | solution.py:876

commit v3 on v2

--- a/solution.py
+++ b/solution.py
@@ -283,9 +283,9 @@
 
 ROWS = 88
 STACK = 4
-PARTS = 2
+PARTS = 1
 LATE = 2
-GROUP = 4
+GROUP = 16
 FEAT = 80
 NT = (((1,), (1,)), ((), ()))
 

time: 28.9 us -> 28 us (0.969)
  Pallas kernels: 27.5 us -> 26.6 us
    pallas_call x1, Pallas kernels: 25.2 us -> 24.3 us  [run_step(): pl.pallas_call(step_kernel, out_shape=(pltpu.VMEM((rows, width), bf16), p...]
where the time goes in v3:
time: 28 us; the launch traced here: 27.9 us
  Pallas kernels  26.6 us (95%)
  between operations  1.29 us (5%)
    pallas_call x1, Pallas kernels, run_step(): pl.pallas_call(step_kernel, out_shape=(pltpu.VMEM((rows, width), bf16), p...  24.3 us
    pallas_call x1, Pallas kernels, deliver(): pl.pallas_call(deliver_kernel, out_shape=[jax.ShapeDtypeStruct(a.shape, a...  2.28 us

profile of v3, /device:TPU:0, one launch (start us, length us, event | category | flops | bytes accessed | tf_op | source)
XLA Modules:
  0.0 27.9 jit_solution(11856307768163332645)
XLA Ops:
  1.3 24.3 %step.1 = (bf16[24,384]{1,0:T(8,128)(2,1)S(1)}, f32[3,3,24]{2,1,0:T(4,128)S(1)}, f32[3,24]{1,0:T(4,128)S(1)}, bf16[24,384,128]{2,1,0:T(8,128)(2,1)S(1)}, bf16[2,...) custom-call(f32[16]{0:T(128)} %refs_0_.1, ...), custom_call_target="tpu_custom_call" | custom-call | tf_op jit(solution)/shard_map/step/pallas_call | solution.py:970
  25.6 2.3 %deliver.1 = (bf16[24,384]{1,0:T(8,128)(2,1)}, f32[3,3,24]{2,1,0:T(4,128)}, f32[3,24]{1,0:T(4,128)}, bf16[24,384,128]{2,1,0:T(8,128)(2,1)}) custom-call(bf16[24,384]{1,0:T(8,128)(2,1)S(1)} %get-tuple-element.12.single, f32[3,3,24]{2,1,0:T(4,128)S(1)} %get-tuple-element.13.rot, f32[3,24]{1,0:T(4,128)S(1)} %get-tuple-element.14.trans, ...), custom_call_target="tpu_custom_call" | custom-call | tf_op jit(solution)/shard_map/deliver/pallas_call | solution.py:876
